TPU v7x, 32 devices: a whole 2x2x4 slice. The times are simulated.
32 devices in a mesh: seq: 2 (over y), exp: 8 (over z, x), enc: 2 (over core).
Axes of the slice: x: 2, y: 2, z: 4, core: 2. Of those that a mesh axis runs over, the one named last changes fastest.
Arguments:
- patches: bfloat16 [8, 4, 272, 1152], P('exp', ('seq', 'enc')), may hold values from -6 to 6
- image_counts: int32 [8, 4], P('exp'), may hold values from 1 to 68, 256 in all within a row
- image_order: int32 [8, 4], P('exp'), may hold values from 0 to 3, each once within a row
- w_merge: bfloat16 [4608, 3456], P(None, ('seq', 'enc')), may hold values from -0.09375 to 0.09375
- w_proj_out: bfloat16 [2, 2, 864, 7168], P(None, 'enc', None, 'seq'), may hold values from -0.109375 to 0.109375
- routes: int32 [2048, 8], P(('exp', 'enc')), may hold values from 0 to 383, all different within a row; in each aligned block of 128 rows (0 to 127, 128 to 255, ...) at most 3 rows name the same one
- route_weight: float32 [2048, 8], P(('exp', 'enc')), may hold values from 0.2 to 1
- expert_place: int32 [384], replicated, may hold values from -1 to 7, as said below
- w_gate: bfloat16 [8, 7168, 1024], P('exp', None, 'seq'), may hold values from -0.0625 to 0.0625
- w_up: bfloat16 [8, 7168, 1024], P('exp', None, 'seq'), may hold values from -0.0625 to 0.0625
- w_down: bfloat16 [8, 1024, 7168], P('exp', 'seq'), may hold values from -0.1875 to 0.1875
Outputs:
- hidden_out: bfloat16 [2048, 7168], P(('exp', 'enc'), 'seq')
- expert_load: float32 [8, 2], P('exp', 'enc')
Inputs may be any that keep to these rules, and one draw needn't show every extreme that they name: `image_counts`: in each row the counts sum to 256 and the largest is exactly 68. `image_order`: each row is a permutation of 0 to 3. `routes`: each row names 8 different experts; among the 128 rows of one device no expert is named by more than 3 rows, a bound that some block reaches. `expert_place`: each of 0 to 7 appears exactly once; every other entry is -1.
All inputs are finite; a program needn't handle non-finite values.
Results may differ from a plain program's by a relative error of at most 0.014.
Values may be sent and summed in bfloat16 or wider, within the bound.
A program may use at most 128 MiB of HBM per device.

v0:
```python
import jax
import jax.numpy as jnp
from jax import lax
from jax.sharding import PartitionSpec as P

D = 7168
ALL_EXPERTS = 384
TOP = 8
MERGE = 4
CAP = 3


def layer_norm(values):
    centre_mean = jnp.mean(values, axis=-1, keepdims=True)
    centred = values - centre_mean
    variance = jnp.mean(centred * centred, axis=-1, keepdims=True)
    return centred * lax.rsqrt(variance + 1e-06)


def sequence_rows(counts, order, seq_len, image_cap):
    shard_total = counts.shape[0]
    shard_ids = jnp.arange(shard_total, dtype=jnp.int32)
    picked = (order[:, None] == shard_ids[None, :]).astype(jnp.int32)
    ordered = jnp.sum(picked * counts[None, :], axis=1)
    run_ends = jnp.cumsum(ordered)
    run_starts = run_ends - ordered
    position = jnp.arange(seq_len, dtype=jnp.int32)
    image_slot = jnp.sum((position[:, None] >= run_ends[None, :]).astype(jnp.int32), axis=1)
    selected = (image_slot[:, None] == shard_ids[None, :]).astype(jnp.int32)
    shard_id = jnp.sum(selected * order[None, :], axis=1)
    first_row = jnp.sum(selected * run_starts[None, :], axis=1)
    return shard_id * image_cap + position - first_row


def slot_table(routes, weights, place, n_dest, cap):
    token_count, top_count = routes.shape
    target = jnp.take(place, routes.reshape(-1), axis=0)
    onehot = (target[:, None] == jnp.arange(n_dest, dtype=jnp.int32)[None, :]).astype(jnp.int32)
    rank_here = jnp.sum((jnp.cumsum(onehot, axis=0) - 1) * onehot, axis=1)
    slot_id = jnp.where(target >= 0, target * cap + rank_here, -1)
    matches = slot_id[None, :] == jnp.arange(n_dest * cap, dtype=jnp.int32)[:, None]
    token_of = jnp.arange(token_count * top_count, dtype=jnp.int32) // top_count
    slot_tok = jnp.sum(jnp.where(matches, token_of[None, :], 0), axis=1)
    live_slot = jnp.any(matches, axis=1)
    mixing = jnp.where(matches, weights.reshape(-1)[None, :], jnp.zeros((), weights.dtype))
    mixing = jnp.sum(mixing.reshape(n_dest * cap, token_count, top_count), axis=2)
    return (slot_tok, live_slot, mixing)


def shards(
    patches,
    image_counts,
    image_order,
    w_merge,
    w_proj_out,
    routes,
    route_weight,
    expert_place,
    w_gate,
    w_up,
    w_down,
):
    seq_count = lax.axis_size("seq")
    enc_count = lax.axis_size("enc")
    exp_count = lax.axis_size("exp")
    image_cap = patches.shape[2] // MERGE
    vit_width = patches.shape[3]
    token_count = routes.shape[0]
    seq_len = token_count * enc_count
    columns = w_proj_out.shape[3]
    unit_count = w_merge.shape[1]
    unit_block = w_proj_out.shape[2]
    piece = lax.all_gather(patches, ("seq", "enc"), axis=1, tiled=True)
    shard_count = piece.shape[1]
    normed = layer_norm(piece[0].astype(jnp.float32)).astype(jnp.bfloat16)
    merged = normed.reshape(shard_count * image_cap, MERGE * vit_width)
    inner_act = jax.nn.gelu(
        jnp.dot(merged, w_merge, preferred_element_type=jnp.float32), approximate=False
    )
    inner_all = inner_act.astype(jnp.bfloat16).reshape(1, shard_count, image_cap, unit_count)
    placed = jnp.take(
        inner_all.reshape(-1, unit_count),
        sequence_rows(image_counts[0], image_order[0], seq_len, image_cap),
        axis=0,
    )
    weight_rows = w_proj_out.reshape(seq_count * unit_block, columns)
    partial_out = jnp.dot(
        lax.all_gather(placed, "seq", axis=1, tiled=True),
        weight_rows,
        preferred_element_type=jnp.float32,
    )
    x_cols = lax.psum_scatter(
        partial_out.astype(jnp.bfloat16), "enc", scatter_dimension=0, tiled=True
    )
    slot_tok, live_slot, mixing = slot_table(routes, route_weight, expert_place, exp_count, CAP)
    live_flags = live_slot.astype(jnp.bfloat16).reshape(exp_count, CAP)
    gate_w = w_gate[0]
    up_w = w_up[0]
    slot_rows = jnp.where(
        live_slot[:, None], jnp.take(x_cols, slot_tok, axis=0), jnp.zeros((), jnp.bfloat16)
    )
    arrived, flags_in = (
        lax.all_to_all(
            slot_rows.reshape(exp_count, CAP, columns),
            "exp",
            split_axis=0,
            concat_axis=0,
            tiled=True,
        ),
        lax.all_to_all(live_flags, "exp", split_axis=0, concat_axis=0, tiled=True),
    )
    piece = lax.all_gather(arrived, "seq", axis=2, tiled=True)
    flattened = piece.reshape(exp_count * CAP, piece.shape[2])
    gate_sum = jnp.dot(flattened, gate_w, preferred_element_type=jnp.float32)
    up_sum = jnp.dot(flattened, up_w, preferred_element_type=jnp.float32)
    squares = jnp.sum(jnp.square(flattened.astype(jnp.float32)), axis=1)
    inv_rms = lax.rsqrt(squares / D + 1e-06)[:, None]
    hidden = (jax.nn.silu(gate_sum * inv_rms) * (up_sum * inv_rms)).astype(jnp.bfloat16)
    down_part = jnp.dot(hidden, w_down[0], preferred_element_type=jnp.float32)
    outputs = lax.psum_scatter(
        down_part.astype(jnp.bfloat16), "seq", scatter_dimension=1, tiled=True
    )
    returned = lax.all_to_all(
        outputs.reshape(exp_count, CAP, columns), "exp", split_axis=0, concat_axis=0, tiled=True
    )
    combined = jnp.dot(
        mixing.T,
        returned.reshape(exp_count * CAP, columns).astype(jnp.float32),
        precision=lax.Precision.HIGHEST,
    )
    hidden_out = (x_cols.astype(jnp.float32) + combined).astype(jnp.bfloat16)
    expert_load = jnp.sum(flags_in.astype(jnp.float32)) * (
        ALL_EXPERTS / (exp_count * token_count * TOP)
    )
    return (hidden_out, expert_load.reshape(1, 1))


def solution(mesh):
    in_specs = (
        P("exp", ("seq", "enc"), None, None),
        P("exp", None),
        P("exp", None),
        P(None, ("seq", "enc")),
        P(None, "enc", None, "seq"),
        P(("exp", "enc"), None),
        P(("exp", "enc"), None),
        P(),
        P("exp", None, "seq"),
        P("exp", None, "seq"),
        P("exp", "seq", None),
    )
    out_specs = (P(("exp", "enc"), "seq"), P("exp", "enc"))
    return jax.shard_map(shards, mesh=mesh, in_specs=in_specs, out_specs=out_specs, check_vma=False)
```

profile of v0, /device:TPU:0, one launch (start us, length us, event | category | flops | bytes accessed | tf_op | source)
XLA Modules:
  0.0 182.1 jit_solution(15759461319029678871)
XLA Ops:
  7.2 0.7 all-gather.2.cloned.1.call-update
  8.0 0.9 select_reduce_fusion.4
  9.1 0.7 select_reduce_fusion.3
  9.9 27.3 %all-gather.2.cloned.1.call-done = bf16[1,4,272,1152]{3,2,0,1:T(8,128)(2,1)} async-done(((bf16[1,1,272,1152]{3,2,0,1:T(8,128)(2,1)}), bf16[1,4,272,1152]{3,2,0,1:T(8,128)(2,1)}) %all-gather.2.cloned.1.call-update) | async-done | bytes 2506768 | tf_op jit(solution)/shard_map/all_gather | solution.py:73
  37.2 2.1 %convert_reduce_fusion = f32[4,272]{1,0:T(4,128)S(1)} fusion(bf16[1,4,272,1152]{3,2,0,1:T(8,128)(2,1)} %all-gather.2.cloned.1.call-done), kind=kLoop, calls=%fused_computation.17 | loop fusion | flops 2505664 | bytes 2511104 | tf_op jit(solution)/shard_map/reduce_sum | solution.py:14
  39.3 2.5 %fusion.6 = f32[4,272]{1,0:T(4,128)S(1)} fusion(bf16[1,4,272,1152]{3,2,0,1:T(8,128)(2,1)} %all-gather.2.cloned.1.call-done, f32[4,272]{1,0:T(4,128)S(1)} %broadcast_multiply_fusion), kind=kLoop, calls=%fused_computation.12 | loop fusion | flops 5012416 | bytes 2515456 | tf_op jit(solution)/shard_map/reduce_sum | solution.py:16
  41.9 2.7 %mul.125 = f32[4,272,1152]{2,1,0:T(8,128)} broadcast(f32[4,272]{1,0:T(4,128)S(1)} %add_rsqrt_fusion), dimensions={0,1} | broadcast | bytes 5017856 | tf_op jit(solution)/shard_map/mul | solution.py:17
  44.5 5.8 %mul.126 = f32[272,4608]{1,0:T(8,128)} reshape(f32[4,272,1152]{2,1,0:T(8,128)} %mul.125) | data formatting | bytes 10027008 | tf_op jit(solution)/shard_map/mul | solution.py:17
  50.4 2.7 %sub.50 = f32[4,272,1152]{2,1,0:T(8,128)} broadcast(f32[4,272]{1,0:T(4,128)S(1)} %broadcast_multiply_fusion), dimensions={0,1} | broadcast | bytes 5017856 | tf_op jit(solution)/shard_map/sub | solution.py:15
  53.1 6.0 %sub.51 = f32[272,4608]{1,0:T(8,128)} reshape(f32[4,272,1152]{2,1,0:T(8,128)} %sub.50) | data formatting | bytes 10027008 | tf_op jit(solution)/shard_map/sub | solution.py:15
  59.1 3.0 %reshape.308 = f32[272,4608]{1,0:T(8,128)} reshape(bf16[1,4,272,1152]{3,2,0,1:T(8,128)(2,1)S(1)} %copy-done.1) | data formatting | bytes 7520256 | tf_op jit(solution)/shard_map/convert_element_type | solution.py:75
  62.1 12.3 %fusion.23 = bf16[272,864]{1,0:T(8,128)(2,1)S(1)} fusion(bf16[4608,864]{0,1:T(8,128)(2,1)} %param.14, f32[272,4608]{1,0:T(8,128)} %mul.126, f32[272,4608]{1,0:T(8,128)} %reshape.308, f32[272,4608]{1,0:T(8,128)} %sub.51), kind=kOutput, calls=%fused_computation.25 | convolution fusion | flops 2184869376 | bytes 23473152 | tf_op jit(solution)/shard_map/dot_general | solution.py:78
  74.4 1.2 gather_fusion
  75.9 13.0 %all_gather.10 = bf16[256,1728]{0,1:T(8,128)(2,1)S(1)} all-gather(bf16[256,864]{0,1:T(8,128)(2,1)S(1)} %copy.49), channel_id=1, replica_groups=mesh['seq'=2,'exp'=8,'enc'=2] {'seq'}, dimensions={1}, use_global_device_ids=true | all-gather | bytes 1327104 | tf_op jit(solution)/shard_map/all_gather | solution.py:88
  88.9 9.2 %convolution_convert_fusion.1 = bf16[256,3584]{1,0:T(8,128)(2,1)} fusion(bf16[256,1728]{0,1:T(8,128)(2,1)S(1)} %all_gather.10, bf16[1728,3584]{1,0:T(8,128)(2,1)} %bitcast.69), kind=kOutput, calls=%fused_computation.9 | convolution fusion | flops 3171811328 | bytes 15106048 | tf_op jit(solution)/shard_map/dot_general | solution.py:87
  98.8 6.9 %gather_fusion.1 = s32[1024]{0:T(1024)S(1)} fusion(s32[384]{0:T(512)S(1)} %copy-done, s32[1024]{0:T(1024)S(1)} %broadcast_clamp_fusion), kind=kCustom, calls=%fused_computation.1 | custom fusion | bytes 12288 | tf_op jit(solution)/shard_map/jit(_take)/gather | solution.py:37
  105.7 2.3 %reduce-window.18 = s32[8,8,128]{2,1,0:T(8,128)S(1)} reduce-window(s32[8,8,128]{2,1,0:T(8,128)S(1)} %fusion.41, s32[]{:T(128)} %constant.50.clone.1), window={size=1x1x128 pad=0_0x0_0x127_0}, to_apply=%region_8.9 | reduce-window | flops 1040384 | bytes 65540 | tf_op jit(solution)/shard_map/reduce-window.1
  109.0 2.1 %gather_fusion.2 = bf16[24,3584]{1,0:T(8,128)(2,1)S(1)} fusion(bf16[128,3584]{1,0:T(8,128)(2,1)} %reduce-scatter.3.cloned.1.call-done, s32[1024]{0:T(1024)S(1)} %pad_clamp_fusion), kind=kCustom, calls=%fused_computation.2 | custom fusion | bytes 344160 | tf_op jit(solution)/shard_map/jit(_take)/gather | solution.py:100
  111.5 13.3 %all_to_all.16 = bf16[8,3,3584]{2,1,0:T(4,128)(2,1)S(1)} all-to-all(bf16[8,3,3584]{2,1,0:T(4,128)(2,1)S(1)} %select_select_fusion), channel_id=1, replica_groups=mesh['seq'=2,'exp'=8,'enc'=2] {'exp'}, dimensions={0} | all-to-all | bytes 344064 | tf_op jit(solution)/shard_map/all_to_all | solution.py:103
  124.8 6.7 %all_gather.11 = bf16[8,3,7168]{2,1,0:T(4,128)(2,1)S(1)} all-gather(bf16[8,3,3584]{2,1,0:T(4,128)(2,1)S(1)} %all_to_all.16), channel_id=1, replica_groups=mesh['seq'=2,'exp'=8,'enc'=2] {'seq'}, dimensions={2}, use_global_device_ids=true | all-gather | bytes 516096 | tf_op jit(solution)/shard_map/all_gather | solution.py:112
  131.5 0.3 reshape.304
  131.8 0.3 multiply_reduce_fusion
  132.2 4.1 %fusion.9 = f32[24,512]{1,0:T(8,128)S(1)} fusion(bf16[24,7168]{1,0:T(8,128)(2,1)S(1)} %reshape.304, bf16[1,7168,512]{2,1,0:T(8,128)(2,1)} %param.19, f32[24]{0:T(128)S(1)} %rsqrt.20), kind=kOutput, calls=%fused_computation.19 | convolution fusion | flops 176173056 | bytes 7733344 | tf_op jit(solution)/shard_map/dot_general | solution.py:114
  136.4 8.1 %convolution_convert_fusion = bf16[24,7168]{1,0:T(8,128)(2,1)} fusion(bf16[1,512,7168]{2,1,0:T(8,128)(2,1)} %param.21, bf16[24,7168]{1,0:T(8,128)(2,1)S(1)} %reshape.304, bf16[1,7168,512]{2,1,0:T(8,128)(2,1)} %param.20, f32[24,512]{1,0:T(8,128)S(1)} %fusion.9, f32[24]{0:T(128)S(1)} %rsqrt.20), kind=kOutput, calls=%fused_computation.3 | convolution fusion | flops 352579584 | bytes 15417440 | tf_op jit(solution)/shard_map/dot_general | solution.py:119
  144.6 0.7 reshape.334
  145.2 4.3 %all-to-all-start.2 = ((bf16[8,1,3]{2,1,0:T(2,128)(2,1)}), bf16[8,1,3]{2,1,0:T(2,128)(2,1)S(1)}, u32[]{:S(2)}, u32[]{:S(2)}) async-start(bf16[8,1,3]{2,1,0:T(2,128)(2,1)} %reshape.334), calls=%async_computation.4 | async-start | bytes 8192 | tf_op jit(solution)/shard_map/all_to_all | solution.py:110
  149.8 7.1 %reduce-scatter.5.cloned.1.call-done = bf16[24,3584]{1,0:T(8,128)(2,1)} async-done(((bf16[24,7168]{1,0:T(8,128)(2,1)}), bf16[24,3584]{1,0:T(8,128)(2,1)}) %reduce-scatter.5.cloned.1.call-update) | async-done | bytes 172048 | tf_op jit(solution)/shard_map/reduce_scatter | solution.py:120
  156.9 1.7 reshape.305
  158.6 5.5 %all-to-all-start.1 = ((bf16[8,3,3584]{2,1,0:T(4,128)(2,1)}), bf16[8,3,3584]{2,1,0:T(4,128)(2,1)S(1)}, u32[]{:S(2)}, u32[]{:S(2)}) async-start(bf16[8,3,3584]{2,1,0:T(4,128)(2,1)} %reshape.305), calls=%async_computation.3 | async-start | bytes 458752 | tf_op jit(solution)/shard_map/all_to_all | solution.py:123
  164.2 0.6 convert_reduce_fusion.1
  165.5 6.9 %all-to-all-done.1 = bf16[8,3,3584]{2,1,0:T(4,128)(2,1)S(1)} async-done(((bf16[8,3,3584]{2,1,0:T(4,128)(2,1)}), bf16[8,3,3584]{2,1,0:T(4,128)(2,1)S(1)}, u32[]{:S(2)}, u32[]{:S(2)}) %all-to-all-start.1) | async-done | bytes 172064 | tf_op jit(solution)/shard_map/all_to_all | solution.py:123
  172.6 1.9 %fusion.7 = bf16[128,3584]{1,0:T(8,128)(2,1)} fusion(f32[24,128]{1,0:T(8,128)S(1)} %select_reduce_fusion.1, bf16[24,3584]{1,0:T(8,128)(2,1)S(1)} %reshape.306, bf16[128,3584]{1,0:T(8,128)(2,1)S(1)} %copy-done.2), kind=kOutput, calls=%fused_computation.15 | convolution fusion | flops 133496832 | bytes 2019328 | tf_op jit(solution)/shard_map/dot_general | solution.py:126
  (61 shorter events, 3.3 us)
Async XLA Ops:
  7.2 91.7 %copy-start = (s32[384]{0:T(512)S(1)}, s32[384]{0:T(512)}, u32[]{:S(2)}) copy-start(s32[384]{0:T(512)} %param.18) | copy-start | bytes 4612
  7.2 30.0 %all-gather.2.cloned.1.call-start = ((), (), s32[]{:S(2)}) async-start(), calls=%async_computation.5 | async-start | bytes 3133440 | tf_op jit(solution)/shard_map/all_gather | solution.py:73
  7.9 101.1 %reduce-scatter.3.cloned.1.call-start = ((), (), s32[]{:S(2)}) async-start(), calls=%async_computation.6 | async-start | bytes 2752512 | tf_op jit(solution)/shard_map/reduce_scatter | solution.py:92
  53.1 6.0 %copy-start.1 = (bf16[1,4,272,1152]{3,2,0,1:T(8,128)(2,1)S(1)}, bf16[1,4,272,1152]{3,2,0,1:T(8,128)(2,1)}, u32[]{:S(2)}) copy-start(bf16[1,4,272,1152]{3,2,0,1:T(8,128)(2,1)} %all-gather.2.cloned.1.call-done) | copy-start | bytes 7520260
  88.9 9.5 %copy-start.3 = (s32[128,8]{0,1:T(8,128)S(1)}, s32[128,8]{0,1:T(8,128)}, u32[]{:S(2)}) copy-start(s32[128,8]{0,1:T(8,128)} %param.16) | copy-start | bytes 12292
  98.2 58.8 %reduce-scatter.5.cloned.1.call-start = ((), (), s32[]{:S(2)}) async-start(), calls=%async_computation.7 | async-start | bytes 516096 | tf_op jit(solution)/shard_map/reduce_scatter | solution.py:120
  136.3 27.8 %copy-start.4 = (f32[128,8]{0,1:T(8,128)S(1)}, f32[128,8]{0,1:T(8,128)}, u32[]{:S(2)}) copy-start(f32[128,8]{0,1:T(8,128)} %param.17) | copy-start | bytes 12292
  136.3 36.2 %copy-start.2 = (bf16[128,3584]{1,0:T(8,128)(2,1)S(1)}, bf16[128,3584]{1,0:T(8,128)(2,1)}, u32[]{:S(2)}) copy-start(bf16[128,3584]{1,0:T(8,128)(2,1)} %reduce-scatter.3.cloned.1.call-done) | copy-start | bytes 2752516
  145.2 13.4 %all-to-all-start.2 = ((bf16[8,1,3]{2,1,0:T(2,128)(2,1)}), bf16[8,1,3]{2,1,0:T(2,128)(2,1)S(1)}, u32[]{:S(2)}, u32[]{:S(2)}) async-start(bf16[8,1,3]{2,1,0:T(2,128)(2,1)} %reshape.334), calls=%async_computation.4 | async-start | bytes 8192 | tf_op jit(solution)/shard_map/all_to_all | solution.py:110
  158.6 13.8 %all-to-all-start.1 = ((bf16[8,3,3584]{2,1,0:T(4,128)(2,1)}), bf16[8,3,3584]{2,1,0:T(4,128)(2,1)S(1)}, u32[]{:S(2)}, u32[]{:S(2)}) async-start(bf16[8,3,3584]{2,1,0:T(4,128)(2,1)} %reshape.305), calls=%async_computation.3 | async-start | bytes 458752 | tf_op jit(solution)/shard_map/all_to_all | solution.py:123
Sparse Core Ops, SparseCore 0:
  9.5 27.5 all-gather.1
  98.3 9.3 reduce-scatter.2
  144.7 12.1 reduce-scatter.4
where the time goes:
time: 183 us; the launch traced here: 182 us
  waiting for transfers between devices  42.1 us (23%)
  matrix products  35.7 us (20%)
  local copies, waits for them, and re-layouts  34.8 us (19%)
  blocking collectives  33 us (18%)
  between operations  15.8 us (9%)
  other arithmetic  10.7 us (6%)
  starting transfers between devices  10.1 us (6%)
    all_gather x1, waiting for transfers between devices, shards(): piece = lax.all_gather(patches, ('seq', 'enc'), axis=1, tiled=True)  27.3 us
    all_to_all x1, blocking collectives, shards(): lax.all_to_all(slot_rows.reshape(exp_count, CAP, columns), 'exp', split_a...  13.3 us
    all_gather x1, blocking collectives, shards(): lax.all_gather(placed, 'seq', axis=1, tiled=True)  13 us
    dot_general x1, matrix products, shards(): jnp.dot(merged, w_merge, preferred_element_type=jnp.float32)  12.3 us
    dot_general x1, matrix products, shards(): jnp.dot(lax.all_gather(placed, 'seq', axis=1, tiled=True), weight_rows, p...  9.24 us
    sub x2, local copies, waits for them, and re-layouts, layer_norm(): centred = values - centre_mean  8.7 us
    mul x2, local copies, waits for them, and re-layouts, layer_norm(): return centred * lax.rsqrt(variance + 1e-06)  8.52 us
    dot_general x1, matrix products, shards(): down_part = jnp.dot(hidden, w_down[0], preferred_element_type=jnp.float32)  8.13 us
  transfers between devices with their start and end apart: 5, of which 3 were waited for; matrix products, arithmetic and copies ran while one was open for 9% of the time, Pallas kernels for 0%

commit v1 on v0

v1 whole, which is shorter than its diff:
```python
import functools

import jax
import jax.numpy as jnp
from jax import lax
from jax.experimental import pallas as pl
from jax.experimental.pallas import tpu as pltpu
from jax.sharding import PartitionSpec as P

MERGE = 4
CAP = 3
PIECE = 4
GROUP = 8
BF = jnp.bfloat16
F32 = jnp.float32
I32 = jnp.int32
MESH = pl.DeviceIdType.MESH


def up(value, step):
    return -(-value // step) * step


def iota(shape, axis):
    return lax.broadcasted_iota(I32, shape, axis)


def mm(a, b):
    return jnp.dot(a, b, preferred_element_type=F32)


def kernel(
    dims,
    counts_ref, order_ref, patches_ref, wm_hbm, w2_hbm, routes_ref, weight_ref, place_ref,
    wg_hbm, wu_hbm, wd_hbm,
    out_ref, load_ref,
    raw, nb, wm, w2, wg, wu, wd, acc1, ib, place_mat, acc2, psend, precv, xbuf,
    slot_send, rs, lf, dsend, drecv, ysend, yrecv, mix, gsel, gcnt,
    raw_sem, wm_sem, w2_sem, wx_sem,
    ny_s, ny_r, nc_s, nc_r, ib_s, ib_r, ps_s, ps_r, sl_s, sl_r, fw_s, fw_r, dn_s, dn_r, bk_s, bk_r,
    own_sem,
):
    ns, ne, nc_enc, cap_img, rp, wr, vit, units, cols, chunk, tok, top, n_all, hid = dims
    nchunk = cols // chunk
    s, e, c = lax.axis_index("seq"), lax.axis_index("exp"), lax.axis_index("enc")
    other = lax.rem(c + 1, nc_enc)

    def to_seq(j):
        return {"seq": lax.rem(s + j, ns)}

    def from_seq(j):
        return lax.rem(s + ns - j, ns)

    core = {"enc": other}

    def to_exp(k):
        return {"exp": lax.rem(e + k, ne)}

    def remote(src, dst, send, recv, dev):
        return pltpu.make_async_remote_copy(
            src_ref=src, dst_ref=dst, send_sem=send, recv_sem=recv, device_id=dev,
            device_id_type=MESH,
        )

    raw_copy = pltpu.make_async_copy(patches_ref.at[0, 0], raw, raw_sem)
    raw_copy.start()
    wm_copies = [
        pltpu.make_async_copy(
            wm_hbm.at[pl.ds(m * vit, vit)], wm.at[pl.ds(m * vit, vit)], wm_sem.at[m]
        )
        for m in range(MERGE)
    ]
    for cp in wm_copies:
        cp.start()
    w2_copies = []
    for j in range(ns):
        b = from_seq(j)
        w2_copies.append(pltpu.make_async_copy(w2_hbm.at[b, 0], w2.at[b], w2_sem.at[j]))
    for cp in w2_copies:
        cp.start()
    wx_copies = [
        pltpu.make_async_copy(wg_hbm.at[0], wg, wx_sem.at[0]),
        pltpu.make_async_copy(wu_hbm.at[0], wu, wx_sem.at[1]),
        pltpu.make_async_copy(wd_hbm.at[0], wd, wx_sem.at[2]),
    ]
    for cp in wx_copies:
        cp.start()

    barrier = pltpu.get_barrier_semaphore()
    for j in range(1, ns):
        pl.semaphore_signal(barrier, inc=1, device_id=to_seq(j), device_id_type=MESH)
    pl.semaphore_signal(barrier, inc=1, device_id=core, device_id_type=MESH)
    for k in range(1, ne):
        pl.semaphore_signal(barrier, inc=1, device_id=to_exp(k), device_id_type=MESH)

    raw_copy.wait()
    values = raw[...].astype(F32)
    centred = values - jnp.mean(values, axis=1, keepdims=True)
    variance = jnp.mean(centred * centred, axis=1, keepdims=True)
    normed = (centred * lax.rsqrt(variance + 1e-06)).astype(BF)
    rows_in = cap_img * MERGE
    k_i, r_i = iota((rp, rows_in), 0), iota((rp, rows_in), 1)
    for m in range(MERGE):
        pick = jnp.where((k_i < cap_img) & (r_i == k_i * MERGE + m), 1.0, 0.0).astype(BF)
        nb[s, c, m] = mm(pick, normed).astype(BF)

    pl.semaphore_wait(barrier, ns - 1 + 1 + ne - 1)

    def nb_at(p, cc, m):
        return nb.at[p, cc, m, pl.ds(0, wr)]

    pending = []
    for m in range(MERGE):
        for j in range(1, ns):
            cp = remote(nb_at(s, c, m), nb_at(s, c, m), ny_s.at[j, m], ny_r.at[j, m], to_seq(j))
            cp.start()
            pending.append(cp)
        cp = remote(nb_at(s, c, m), nb_at(s, c, m), nc_s.at[0, m], nc_r.at[0, m], core)
        cp.start()
        pending.append(cp)

    live = lax.rem(iota((nc_enc * rp, 1), 0), rp) < cap_img

    def finish_inner(p):
        a = acc1[...]
        inner = 0.5 * a * (1.0 + lax.erf(a * 0.7071067811865476))
        ib[s, p] = jnp.where(live, inner, 0.0).astype(BF)

    def send_inner(p, j0):
        for j in range(1, ns):
            cp = remote(ib.at[s, p], ib.at[s, p], ib_s.at[j, j0], ib_r.at[j, j0], to_seq(j))
            cp.start()
            pending.append(cp)

    def mm1(p, m):
        lhs = nb[p, :, m].reshape(nc_enc * rp, vit)
        term = mm(lhs, wm[pl.ds(m * vit, vit), :])
        if m == 0:
            acc1[...] = term
        else:
            acc1[...] += term

    ncol = mix.shape[1] // 3
    place = place_ref[...]
    d_of = iota((ncol, n_all), 0) // GROUP
    held = jnp.where(place == d_of, 1.0, 0.0).astype(BF)
    number = iota((GROUP, n_all), 1)
    contract_last = (((1,), (1,)), ((), ()))
    high = lax.dot_general(
        (number // 16).astype(F32).astype(BF), held, contract_last, preferred_element_type=F32
    )
    low = lax.dot_general(
        lax.rem(number, 16).astype(F32).astype(BF), held, contract_last,
        preferred_element_type=F32,
    )
    expert = (high * 16.0 + low)[0:1].astype(I32)
    col = iota((1, ncol), 1)
    expert = jnp.where(col < ne * GROUP, expert, -1)
    q_of = lax.rem(col, GROUP)
    named = jnp.zeros((tok, ncol), F32)
    amount = jnp.zeros((tok, ncol), F32)
    for k in range(top):
        match = routes_ref[:, k : k + 1] == expert
        named = jnp.where(match, 1.0, named)
        amount = amount + jnp.where(match, weight_ref[:, k : k + 1], 0.0)
    earlier = jnp.where(iota((tok, tok), 1) < iota((tok, tok), 0), 1.0, 0.0).astype(BF)
    rank = mm(earlier, named.astype(BF))
    chosen = jnp.where((rank == q_of.astype(F32)) & (q_of < CAP), named, 0.0)
    mixing = chosen * amount
    part_a = mixing.astype(BF)
    rest = mixing - part_a.astype(F32)
    part_b = rest.astype(BF)
    part_c = (rest - part_b.astype(F32)).astype(BF)
    mix[:, 0:ncol] = part_a
    mix[:, ncol : 2 * ncol] = part_b
    mix[:, 2 * ncol : 3 * ncol] = part_c
    gsel[...] = jnp.transpose(chosen).astype(BF)
    counted = jnp.transpose(jnp.where(q_of == CAP, named, 0.0))
    gcnt[...] = jnp.broadcast_to(jnp.sum(counted, axis=1, keepdims=True), gcnt.shape)
    lf[...] = jnp.zeros(lf.shape, F32)

    shard_total = ns * nc_enc
    starts, run = [], jnp.int32(0)
    for i in range(shard_total):
        starts.append(run)
        o_i = order_ref[0, i]
        for j in range(shard_total):
            run = run + jnp.where(o_i == j, counts_ref[0, j], 0)
    seq_len = tok * nc_enc
    position = lax.rem(iota((seq_len, rp), 0) + other * tok, seq_len)
    k_row = iota((seq_len, rp), 1)
    for j in range(shard_total):
        first = jnp.int32(0)
        for i in range(shard_total):
            first = first + jnp.where(order_ref[0, i] == j, starts[i], 0)
        hit = (position - first == k_row) & (k_row < counts_ref[0, j])
        place_mat[j] = jnp.where(hit, 1.0, 0.0).astype(BF)

    for m in range(MERGE):
        wm_copies[m].wait()
        remote(
            nb_at(s, other, m), nb_at(s, other, m), nc_s.at[0, m], nc_r.at[0, m], core
        ).wait_recv()
        mm1(s, m)
    finish_inner(s)
    send_inner(s, 0)
    for j in range(1, ns):
        p = from_seq(j)
        for m in range(MERGE):
            remote(
                nb_at(p, c, m), nb_at(p, c, m), ny_s.at[j, m], ny_r.at[j, m], to_seq(j)
            ).wait_recv()
            cp = remote(nb_at(p, c, m), nb_at(p, c, m), nc_s.at[j, m], nc_r.at[j, m], core)
            cp.start()
            pending.append(cp)
            remote(
                nb_at(p, other, m), nb_at(p, other, m), nc_s.at[j, m], nc_r.at[j, m], core
            ).wait_recv()
            mm1(p, m)
        finish_inner(p)
        send_inner(p, j)

    def placed_of(b):
        total = jnp.zeros((seq_len, units), F32)
        for p in range(ns):
            for cc in range(nc_enc):
                total += mm(place_mat[p * nc_enc + cc], ib[b, p, pl.ds(cc * rp, rp)])
        return total.astype(BF)

    def columns_at(n):
        return pl.ds(pl.multiple_of(n * chunk, chunk), chunk)

    for j in range(ns):
        b = from_seq(j)
        if j > 0:
            for t in range(ns):
                src_p = lax.rem(b + ns - t, ns)
                remote(
                    ib.at[b, src_p], ib.at[b, src_p], ib_s.at[j, t], ib_r.at[j, t], to_seq(j)
                ).wait_recv()
        w2_copies[j].wait()
        placed = placed_of(b)
        for n in range(nchunk):
            term = mm(placed, w2[b, :, n * chunk : (n + 1) * chunk])
            if j > 0:
                term = acc2[n] + term
            if j < ns - 1:
                acc2[n] = term
            else:
                psend[n] = term[0:tok].astype(BF)
                xbuf[n] = term[tok : 2 * tok].astype(BF)
                cp = remote(psend.at[n], precv.at[n], ps_s.at[n], ps_r.at[n], core)
                cp.start()
                pending.append(cp)

    flag_row = lax.rem(iota((ncol, 1), 0), GROUP) == CAP
    for n in range(nchunk):
        remote(psend.at[n], precv.at[n], ps_s.at[n], ps_r.at[n], core).wait_recv()
        x = (xbuf[n].astype(F32) + precv[n].astype(F32)).astype(BF)
        xbuf[n] = x
        rows = jnp.where(flag_row, gcnt[:, 0:1], mm(gsel[...], x))
        for d in range(ne):
            slot_send[d, :, n * chunk : (n + 1) * chunk] = rows[
                d * GROUP : d * GROUP + PIECE
            ].astype(BF)

    for k in range(1, ne):
        dst = lax.rem(e + k, ne)
        cp = remote(slot_send.at[dst], rs.at[s, e], sl_s.at[k], sl_r.at[k], to_exp(k))
        cp.start()
        pending.append(cp)
    own_copy = pltpu.make_async_copy(slot_send.at[e], rs.at[s, e], own_sem.at[0])
    own_copy.start()
    for k in range(ne):
        src = lax.rem(e + ne - k, ne)
        if k == 0:
            own_copy.wait()
        else:
            remote(slot_send.at[e], rs.at[s, src], sl_s.at[k], sl_r.at[k], to_exp(k)).wait_recv()
        for j in range(1, ns):
            cp = remote(rs.at[s, src], rs.at[s, src], fw_s.at[j, k], fw_r.at[j, k], to_seq(j))
            cp.start()
            pending.append(cp)

    rows_e = ne * GROUP
    gate_sum = jnp.zeros((rows_e, hid), F32)
    up_sum = jnp.zeros((rows_e, hid), F32)
    squares = jnp.zeros((rows_e, 1), F32)
    wx_copies[0].wait()
    wx_copies[1].wait()
    for j in range(ns):
        p = from_seq(j)
        if j > 0:
            for k in range(ne):
                src = lax.rem(e + ne - k, ne)
                remote(
                    rs.at[p, src], rs.at[p, src], fw_s.at[j, k], fw_r.at[j, k], to_seq(j)
                ).wait_recv()
        for d in range(ne):
            lf[d * GROUP : d * GROUP + PIECE] = rs[p, d].astype(F32)
        if j == 0:
            tile = lf[:, 0:128]
            flagged = (lax.rem(iota(tile.shape, 0), GROUP) == CAP) & (iota(tile.shape, 1) == 0)
            filled = jnp.where(flagged, tile, 0.0)
            filled = jnp.sum(jnp.sum(filled, axis=1, keepdims=True), axis=0, keepdims=True)
            load_ref[...] = filled * (n_all / (ne * tok * top))
        for n in range(nchunk):
            block = lf[:, n * chunk : (n + 1) * chunk]
            squares = squares + jnp.sum(block * block, axis=1, keepdims=True)
            lhs = block.astype(BF)
            at = pl.ds(pl.multiple_of(p * cols + n * chunk, chunk), chunk)
            gate_sum = gate_sum + mm(lhs, wg[at, :])
            up_sum = up_sum + mm(lhs, wu[at, :])
    inv_rms = lax.rsqrt(squares / (ns * cols) + 1e-06)
    gate = gate_sum * inv_rms
    hidden = (gate / (1.0 + jnp.exp(-gate)) * (up_sum * inv_rms)).astype(BF)
    wx_copies[2].wait()

    for j in list(range(1, ns)) + [0]:
        p = lax.rem(s + j, ns)
        for n in range(nchunk):
            at = pl.ds(pl.multiple_of(p * cols + n * chunk, chunk), chunk)
            term = mm(hidden, wd[:, at])
            for d in range(ne):
                dsend[j, d, :, n * chunk : (n + 1) * chunk] = term[
                    d * GROUP : d * GROUP + PIECE
                ].astype(BF)
        if j > 0:
            cp = remote(dsend.at[j], drecv.at[j], dn_s.at[j], dn_r.at[j], to_seq(j))
            cp.start()
            pending.append(cp)
    for j in range(1, ns):
        remote(dsend.at[j], drecv.at[j], dn_s.at[j], dn_r.at[j], to_seq(j)).wait_recv()
    total = dsend[0].astype(F32)
    for j in range(1, ns):
        total = total + drecv[j].astype(F32)
    ysend[...] = total.astype(BF)
    for k in range(1, ne):
        dst = lax.rem(e + k, ne)
        cp = remote(ysend.at[dst], yrecv.at[e], bk_s.at[k], bk_r.at[k], to_exp(k))
        cp.start()
        pending.append(cp)
    back_copy = pltpu.make_async_copy(ysend.at[e], yrecv.at[e], own_sem.at[1])
    back_copy.start()
    back_copy.wait()
    for k in range(1, ne):
        src = lax.rem(e + ne - k, ne)
        remote(ysend.at[e], yrecv.at[src], bk_s.at[k], bk_r.at[k], to_exp(k)).wait_recv()
    for d in range(ne):
        lf[d * GROUP : d * GROUP + PIECE] = yrecv[d].astype(F32)
    for n in range(nchunk):
        y = lf[:, n * chunk : (n + 1) * chunk].astype(BF)
        if ncol > rows_e:
            y = jnp.concatenate([y, jnp.zeros((ncol - rows_e, chunk), BF)], axis=0)
        combined = mm(mix[...], jnp.concatenate([y, y, y], axis=0))
        out_ref[:, n * chunk : (n + 1) * chunk] = (xbuf[n].astype(F32) + combined).astype(BF)
    for cp in pending:
        cp.wait_send()


def shards(mesh_shape, *args):
    (patches, image_counts, image_order, w_merge, w_proj_out, routes, route_weight,
     expert_place, w_gate, w_up, w_down) = args
    ns, ne, nc = mesh_shape["seq"], mesh_shape["exp"], mesh_shape["enc"]
    rows_in, vit = patches.shape[2:]
    cap_img = rows_in // MERGE
    rp = up(cap_img, 16)
    wr = up(cap_img, 8)
    units = w_merge.shape[1]
    cols = w_proj_out.shape[3]
    tok, top = routes.shape
    n_all = expert_place.shape[0]
    hid = w_gate.shape[2]
    chunk = [w for w in (512, 256, 128) if cols % w == 0][0]
    nchunk = cols // chunk
    ncol = up(ne * GROUP, 128)
    dims = (ns, ne, nc, cap_img, rp, wr, vit, units, cols, chunk, tok, top, n_all, hid)
    anyspec = pl.BlockSpec(memory_space=pl.ANY)
    vmem = pl.BlockSpec(memory_space=pltpu.VMEM)
    smem = pl.BlockSpec(memory_space=pltpu.SMEM)
    dma = pltpu.SemaphoreType.DMA
    V = pltpu.VMEM
    scratch = [
        V((rows_in, vit), BF),
        V((ns, nc, MERGE, rp, vit), BF),
        V((MERGE * vit, units), BF),
        V((ns, units, cols), BF),
        V((ns * cols, hid), BF),
        V((ns * cols, hid), BF),
        V((hid, ns * cols), BF),
        V((nc * rp, units), F32),
        V((ns, ns, nc * rp, units), BF),
        V((ns * nc, tok * nc, rp), BF),
        V((nchunk, tok * nc, chunk), F32),
        V((nchunk, tok, chunk), BF),
        V((nchunk, tok, chunk), BF),
        V((nchunk, tok, chunk), BF),
        V((ne, PIECE, cols), BF),
        V((ns, ne, PIECE, cols), BF),
        V((ne * GROUP, cols), F32),
        V((ns, ne, PIECE, cols), BF),
        V((ns, ne, PIECE, cols), BF),
        V((ne, PIECE, cols), BF),
        V((ne, PIECE, cols), BF),
        V((tok, 3 * ncol), BF),
        V((ncol, tok), BF),
        V((ncol, 128), F32),
        dma, dma((MERGE,)), dma((ns,)), dma((3,)),
        dma((ns, MERGE)), dma((ns, MERGE)), dma((ns, MERGE)), dma((ns, MERGE)),
        dma((ns, ns)), dma((ns, ns)), dma((nchunk,)), dma((nchunk,)),
        dma((ne,)), dma((ne,)), dma((ns, ne)), dma((ns, ne)),
        dma((ns,)), dma((ns,)), dma((ne,)), dma((ne,)),
        dma((2,)),
    ]
    return pl.pallas_call(
        functools.partial(kernel, dims),
        out_shape=(
            jax.ShapeDtypeStruct((tok, cols), BF),
            jax.ShapeDtypeStruct((1, 1), F32),
        ),
        in_specs=[smem, smem, anyspec, anyspec, anyspec, vmem, vmem, vmem] + [anyspec] * 3,
        out_specs=(vmem, vmem),
        scratch_shapes=scratch,
        compiler_params=pltpu.CompilerParams(
            collective_id=0, has_side_effects=True, vmem_limit_bytes=67043328
        ),
        name="step",
    )(
        image_counts, image_order, patches, w_merge, w_proj_out, routes, route_weight,
        expert_place.reshape(1, n_all), w_gate, w_up, w_down,
    )


def solution(mesh):
    in_specs = (
        P("exp", ("seq", "enc"), None, None),
        P("exp", None),
        P("exp", None),
        P(None, ("seq", "enc")),
        P(None, "enc", None, "seq"),
        P(("exp", "enc"), None),
        P(("exp", "enc"), None),
        P(),
        P("exp", None, "seq"),
        P("exp", None, "seq"),
        P("exp", "seq", None),
    )
    out_specs = (P(("exp", "enc"), "seq"), P("exp", "enc"))
    body = functools.partial(shards, dict(mesh.shape))
    return jax.shard_map(body, mesh=mesh, in_specs=in_specs, out_specs=out_specs, check_vma=False)
```

time: 183 us -> 92 us (0.50)
  Pallas kernels: 0 us -> 71.3 us
  waiting for transfers between devices: 42.1 us -> 0 us
  matrix products: 35.7 us -> 0 us
  blocking collectives: 33 us -> 0 us
  local copies, waits for them, and re-layouts: 34.8 us -> 17.7 us
  between operations: 15.8 us -> 2.46 us
  other arithmetic: 10.7 us -> 0 us
  starting transfers between devices: 10.1 us -> 0 us
    pallas_call x0 -> x1, Pallas kernels: none -> 71.3 us  [shards(): pl.pallas_call(functools.partial(kernel, dims), out_shape=(jax.ShapeDtype...]
    dot_general x5 -> x0, matrix products: 35.7 us -> none  [the longest x1 12.3 us: shards(): jnp.dot(merged, w_merge, preferred_element_type=jnp.float32)]
    all_gather x1 -> x0, waiting for transfers between devices: 27.3 us -> none  [shards(): piece = lax.all_gather(patches, ('seq', 'enc'), axis=1, tiled=True)]
    all_gather x2 -> x0, blocking collectives: 19.6 us -> none  [the longest x1 13 us: shards(): lax.all_gather(placed, 'seq', axis=1, tiled=True)]
    unnamed x11 -> x4, local copies, waits for them, and re-layouts: 0.17 us -> 16.5 us
    all_to_all x1 -> x0, blocking collectives: 13.3 us -> none  [shards(): lax.all_to_all(slot_rows.reshape(exp_count, CAP, columns), 'exp', split_a...]
    gather x6 -> x0, local copies, waits for them, and re-layouts: 10.4 us -> none  [the longest x3 7 us: slot_table(): target = jnp.take(place, routes.reshape(-1), axis=0)]
    all_to_all x2 -> x0, starting transfers between devices: 9.79 us -> none  [the longest x1 5.53 us: shards(): lax.all_to_all(outputs.reshape(exp_count, CAP, columns), 'exp', split_axi...]
  transfers between devices with their start and end apart: 5 -> 0, of which waited for: 3 -> 0; matrix products, arithmetic and copies ran while one was open for 9% -> 0% of each run, Pallas kernels for 0% -> 0%
where the time goes in v1:
time: 92 us; the launch traced here: 91.4 us
  Pallas kernels  71.3 us (78%)
  local copies, waits for them, and re-layouts  17.7 us (19%)
  between operations  2.46 us (3%)
    pallas_call x1, Pallas kernels, shards(): pl.pallas_call(functools.partial(kernel, dims), out_shape=(jax.ShapeDtype...  71.3 us
    unnamed x4, local copies, waits for them, and re-layouts  16.5 us

profile of v1, /device:TPU:0, one launch (start us, length us, event | category | flops | bytes accessed | tf_op | source)
XLA Modules:
  0.0 91.4 jit_solution(18174652806856096953)
XLA Ops:
  0.6 1.3 %reshape.7.place_ref = s32[1,384]{1,0:T(1,128)} reshape(s32[384]{0:T(512)} %param.18) | data formatting | bytes 3072 | tf_op jit(solution)/shard_map/reshape | solution.py:430
  1.9 1.4 %copy.14.routes_ref = s32[128,8]{1,0:T(8,128)} copy(s32[128,8]{0,1:T(8,128)} %param.16) | data formatting | bytes 8192 | tf_op args[5]
  3.3 1.4 %copy.15.weight_ref = f32[128,8]{1,0:T(8,128)} copy(f32[128,8]{0,1:T(8,128)} %param.17) | data formatting | bytes 8192 | tf_op args[6]
  4.7 11.5 %copy.13.wm_hbm = bf16[4608,864]{1,0:T(8,128)(2,1)} copy(bf16[4608,864]{0,1:T(8,128)(2,1)} %param.14) | data formatting | bytes 15925248 | tf_op args[3]
  16.2 71.3 %step.1 = (bf16[128,3584]{1,0:T(8,128)(2,1)}, f32[1,1]{1,0:T(1,128)}) custom-call(s32[1,4]{1,0:T(1,128)} %counts_ref.1, s32[1,4]{1,0:T(1,128)} %order_ref.1, bf16[1,1,272,1152]{3,2,1,0:T(8,128)(2,1)} %patches_ref.1, bf16[4608,864]{1,0:T(8,128)(2,1)} %copy.13.wm_hbm, bf16[2,1,864,3584]{3,2,1,0:T(8,128)(2,1)} %w2_hbm.1, s32[128,8]{1,0:T(8,128)} %copy.14.routes_ref, ...), custom_call_target="tpu_custom_call" | custom-call | tf_op jit(solution)/shard_map/step/pallas_call | solution.py:415
  87.5 2.2 %copy.18 = bf16[128,3584]{1,0:T(8,128)(2,1)} copy(bf16[128,3584]{1,0:T(8,128)(2,1)} %get-tuple-element.4) | data formatting | bytes 1835008

commit v2 on v1

--- a/solution.py
+++ b/solution.py
@@ -66,7 +66,7 @@
     raw_copy.start()
     wm_copies = [
         pltpu.make_async_copy(
-            wm_hbm.at[pl.ds(m * vit, vit)], wm.at[pl.ds(m * vit, vit)], wm_sem.at[m]
+            wm_hbm.at[:, pl.ds(m * vit, vit)], wm.at[m], wm_sem.at[m]
         )
         for m in range(MERGE)
     ]
@@ -134,39 +134,32 @@
 
     def mm1(p, m):
         lhs = nb[p, :, m].reshape(nc_enc * rp, vit)
-        term = mm(lhs, wm[pl.ds(m * vit, vit), :])
+        term = lax.dot_general(
+            lhs, wm[m], (((1,), (1,)), ((), ())), preferred_element_type=F32
+        )
         if m == 0:
             acc1[...] = term
         else:
             acc1[...] += term
 
     ncol = mix.shape[1] // 3
-    place = place_ref[...]
+    place = place_ref[...].reshape(1, n_all)
     d_of = iota((ncol, n_all), 0) // GROUP
-    held = jnp.where(place == d_of, 1.0, 0.0).astype(BF)
-    number = iota((GROUP, n_all), 1)
-    contract_last = (((1,), (1,)), ((), ()))
-    high = lax.dot_general(
-        (number // 16).astype(F32).astype(BF), held, contract_last, preferred_element_type=F32
-    )
-    low = lax.dot_general(
-        lax.rem(number, 16).astype(F32).astype(BF), held, contract_last,
-        preferred_element_type=F32,
-    )
-    expert = (high * 16.0 + low)[0:1].astype(I32)
-    col = iota((1, ncol), 1)
-    expert = jnp.where(col < ne * GROUP, expert, -1)
-    q_of = lax.rem(col, GROUP)
-    named = jnp.zeros((tok, ncol), F32)
-    amount = jnp.zeros((tok, ncol), F32)
+    number = iota((ncol, n_all), 1)
+    expert = jnp.sum(jnp.where(place == d_of, number, 0), axis=1, keepdims=True)
+    row = iota((ncol, 1), 0)
+    expert = jnp.where(row < ne * GROUP, expert, -1)
+    q_of = lax.rem(row, GROUP)
+    named = jnp.zeros((ncol, tok), F32)
+    amount = jnp.zeros((ncol, tok), F32)
     for k in range(top):
-        match = routes_ref[:, k : k + 1] == expert
+        match = routes_ref[k : k + 1, :] == expert
         named = jnp.where(match, 1.0, named)
-        amount = amount + jnp.where(match, weight_ref[:, k : k + 1], 0.0)
-    earlier = jnp.where(iota((tok, tok), 1) < iota((tok, tok), 0), 1.0, 0.0).astype(BF)
-    rank = mm(earlier, named.astype(BF))
+        amount = amount + jnp.where(match, weight_ref[k : k + 1, :], 0.0)
+    earlier = jnp.where(iota((tok, tok), 0) < iota((tok, tok), 1), 1.0, 0.0).astype(BF)
+    rank = mm(named.astype(BF), earlier)
     chosen = jnp.where((rank == q_of.astype(F32)) & (q_of < CAP), named, 0.0)
-    mixing = chosen * amount
+    mixing = jnp.transpose(chosen * amount)
     part_a = mixing.astype(BF)
     rest = mixing - part_a.astype(F32)
     part_b = rest.astype(BF)
@@ -174,8 +167,8 @@
     mix[:, 0:ncol] = part_a
     mix[:, ncol : 2 * ncol] = part_b
     mix[:, 2 * ncol : 3 * ncol] = part_c
-    gsel[...] = jnp.transpose(chosen).astype(BF)
-    counted = jnp.transpose(jnp.where(q_of == CAP, named, 0.0))
+    gsel[...] = chosen.astype(BF)
+    counted = jnp.where(q_of == CAP, named, 0.0)
     gcnt[...] = jnp.broadcast_to(jnp.sum(counted, axis=1, keepdims=True), gcnt.shape)
     lf[...] = jnp.zeros(lf.shape, F32)
 
@@ -383,7 +376,7 @@
     scratch = [
         V((rows_in, vit), BF),
         V((ns, nc, MERGE, rp, vit), BF),
-        V((MERGE * vit, units), BF),
+        V((MERGE, units, vit), BF),
         V((ns, units, cols), BF),
         V((ns * cols, hid), BF),
         V((ns * cols, hid), BF),
@@ -426,8 +419,8 @@
         ),
         name="step",
     )(
-        image_counts, image_order, patches, w_merge, w_proj_out, routes, route_weight,
-        expert_place.reshape(1, n_all), w_gate, w_up, w_down,
+        image_counts, image_order, patches, w_merge.T, w_proj_out, routes.T, route_weight.T,
+        expert_place, w_gate, w_up, w_down,
     )
 
 

time: 92 us -> 75.9 us (0.83)
  local copies, waits for them, and re-layouts: 17.7 us -> 2.16 us
    unnamed x4 -> x1, local copies, waits for them, and re-layouts: 16.5 us -> 2.16 us
    reshape x1 -> x0, local copies, waits for them, and re-layouts: 1.28 us -> none  [shards(): expert_place.reshape(1, n_all)]
where the time goes in v2:
time: 75.9 us; the launch traced here: 75.7 us
  Pallas kernels  71.1 us (94%)
  between operations  2.44 us (3%)
  local copies, waits for them, and re-layouts  2.16 us (3%)
    pallas_call x1, Pallas kernels, shards(): pl.pallas_call(functools.partial(kernel, dims), out_shape=(jax.ShapeDtype...  71.1 us
    unnamed x1, local copies, waits for them, and re-layouts  2.16 us

profile of v2, /device:TPU:0, one launch (start us, length us, event | category | flops | bytes accessed | tf_op | source)
XLA Modules:
  0.0 75.7 jit_solution(14970411601090217589)
XLA Ops:
  0.6 71.1 %step.1 = (bf16[128,3584]{1,0:T(8,128)(2,1)}, f32[1,1]{1,0:T(1,128)}) custom-call(s32[1,4]{1,0:T(1,128)} %counts_ref.1, s32[1,4]{1,0:T(1,128)} %order_ref.1, bf16[1,1,272,1152]{3,2,1,0:T(8,128)(2,1)} %patches_ref.1, bf16[864,4608]{1,0:T(8,128)(2,1)} %bitcast.3, bf16[2,1,864,3584]{3,2,1,0:T(8,128)(2,1)} %w2_hbm.1, s32[8,128]{1,0:T(8,128)} %bitcast.4, ...), custom_call_target="tpu_custom_call" | custom-call | tf_op jit(solution)/shard_map/step/pallas_call | solution.py:408
  71.7 2.2 %copy.15 = bf16[128,3584]{1,0:T(8,128)(2,1)} copy(bf16[128,3584]{1,0:T(8,128)(2,1)} %get-tuple-element.4) | data formatting | bytes 1835008

commit v3 on v2

--- a/solution.py
+++ b/solution.py
@@ -86,6 +86,7 @@
     for cp in wx_copies:
         cp.start()
 
+    ib[...] = jnp.zeros(ib.shape, BF)
     barrier = pltpu.get_barrier_semaphore()
     for j in range(1, ns):
         pl.semaphore_signal(barrier, inc=1, device_id=to_seq(j), device_id_type=MESH)
@@ -100,17 +101,14 @@
     normed = (centred * lax.rsqrt(variance + 1e-06)).astype(BF)
     rows_in = cap_img * MERGE
     k_i, r_i = iota((rp, rows_in), 0), iota((rp, rows_in), 1)
+    def nb_at(p, cc, m):
+        return nb.at[p, cc, m, pl.ds(0, wr)]
+
+    pending = []
+    pl.semaphore_wait(barrier, ns - 1 + 1 + ne - 1)
     for m in range(MERGE):
         pick = jnp.where((k_i < cap_img) & (r_i == k_i * MERGE + m), 1.0, 0.0).astype(BF)
         nb[s, c, m] = mm(pick, normed).astype(BF)
-
-    pl.semaphore_wait(barrier, ns - 1 + 1 + ne - 1)
-
-    def nb_at(p, cc, m):
-        return nb.at[p, cc, m, pl.ds(0, wr)]
-
-    pending = []
-    for m in range(MERGE):
         for j in range(1, ns):
             cp = remote(nb_at(s, c, m), nb_at(s, c, m), ny_s.at[j, m], ny_r.at[j, m], to_seq(j))
             cp.start()
@@ -121,14 +119,17 @@
 
     live = lax.rem(iota((nc_enc * rp, 1), 0), rp) < cap_img
 
+    def ib_at(b, p):
+        return ib.at[b, p, :, pl.ds(0, wr)]
+
     def finish_inner(p):
         a = acc1[...]
         inner = 0.5 * a * (1.0 + lax.erf(a * 0.7071067811865476))
-        ib[s, p] = jnp.where(live, inner, 0.0).astype(BF)
+        ib[s, p] = jnp.where(live, inner, 0.0).astype(BF).reshape(nc_enc, rp, units)
 
     def send_inner(p, j0):
         for j in range(1, ns):
-            cp = remote(ib.at[s, p], ib.at[s, p], ib_s.at[j, j0], ib_r.at[j, j0], to_seq(j))
+            cp = remote(ib_at(s, p), ib_at(s, p), ib_s.at[j, j0], ib_r.at[j, j0], to_seq(j))
             cp.start()
             pending.append(cp)
 
@@ -217,7 +218,7 @@
         total = jnp.zeros((seq_len, units), F32)
         for p in range(ns):
             for cc in range(nc_enc):
-                total += mm(place_mat[p * nc_enc + cc], ib[b, p, pl.ds(cc * rp, rp)])
+                total += mm(place_mat[p * nc_enc + cc], ib[b, p, cc])
         return total.astype(BF)
 
     def columns_at(n):
@@ -229,7 +230,7 @@
             for t in range(ns):
                 src_p = lax.rem(b + ns - t, ns)
                 remote(
-                    ib.at[b, src_p], ib.at[b, src_p], ib_s.at[j, t], ib_r.at[j, t], to_seq(j)
+                    ib_at(b, src_p), ib_at(b, src_p), ib_s.at[j, t], ib_r.at[j, t], to_seq(j)
                 ).wait_recv()
         w2_copies[j].wait()
         placed = placed_of(b)
@@ -309,6 +310,12 @@
     hidden = (gate / (1.0 + jnp.exp(-gate)) * (up_sum * inv_rms)).astype(BF)
     wx_copies[2].wait()
 
+    def down_copy(j, n):
+        at = pl.ds(n * chunk, chunk)
+        return remote(
+            dsend.at[j, :, :, at], drecv.at[j, :, :, at], dn_s.at[j, n], dn_r.at[j, n], to_seq(j)
+        )
+
     for j in list(range(1, ns)) + [0]:
         p = lax.rem(s + j, ns)
         for n in range(nchunk):
@@ -318,16 +325,17 @@
                 dsend[j, d, :, n * chunk : (n + 1) * chunk] = term[
                     d * GROUP : d * GROUP + PIECE
                 ].astype(BF)
-        if j > 0:
-            cp = remote(dsend.at[j], drecv.at[j], dn_s.at[j], dn_r.at[j], to_seq(j))
-            cp.start()
-            pending.append(cp)
-    for j in range(1, ns):
-        remote(dsend.at[j], drecv.at[j], dn_s.at[j], dn_r.at[j], to_seq(j)).wait_recv()
-    total = dsend[0].astype(F32)
-    for j in range(1, ns):
-        total = total + drecv[j].astype(F32)
-    ysend[...] = total.astype(BF)
+            if j > 0:
+                cp = down_copy(j, n)
+                cp.start()
+                pending.append(cp)
+    for n in range(nchunk):
+        at = pl.ds(n * chunk, chunk)
+        total = dsend[0, :, :, at].astype(F32)
+        for j in range(1, ns):
+            down_copy(j, n).wait_recv()
+            total = total + drecv[j, :, :, at].astype(F32)
+        ysend[:, :, at] = total.astype(BF)
     for k in range(1, ne):
         dst = lax.rem(e + k, ne)
         cp = remote(ysend.at[dst], yrecv.at[e], bk_s.at[k], bk_r.at[k], to_exp(k))
@@ -382,7 +390,7 @@
         V((ns * cols, hid), BF),
         V((hid, ns * cols), BF),
         V((nc * rp, units), F32),
-        V((ns, ns, nc * rp, units), BF),
+        V((ns, ns, nc, rp, units), BF),
         V((ns * nc, tok * nc, rp), BF),
         V((nchunk, tok * nc, chunk), F32),
         V((nchunk, tok, chunk), BF),
@@ -402,7 +410,7 @@
         dma((ns, MERGE)), dma((ns, MERGE)), dma((ns, MERGE)), dma((ns, MERGE)),
         dma((ns, ns)), dma((ns, ns)), dma((nchunk,)), dma((nchunk,)),
         dma((ne,)), dma((ne,)), dma((ns, ne)), dma((ns, ne)),
-        dma((ns,)), dma((ns,)), dma((ne,)), dma((ne,)),
+        dma((ns, nchunk)), dma((ns, nchunk)), dma((ne,)), dma((ne,)),
         dma((2,)),
     ]
     return pl.pallas_call(

time: 75.9 us -> 73.8 us (0.972)
  Pallas kernels: 71.1 us -> 69 us
    pallas_call x1, Pallas kernels: 71.1 us -> 69 us  [shards(): pl.pallas_call(functools.partial(kernel, dims), out_shape=(jax.ShapeDtype...]
where the time goes in v3:
time: 73.8 us; the launch traced here: 73.6 us
  Pallas kernels  69 us (93%)
  between operations  2.44 us (3%)
  local copies, waits for them, and re-layouts  2.16 us (3%)
    pallas_call x1, Pallas kernels, shards(): pl.pallas_call(functools.partial(kernel, dims), out_shape=(jax.ShapeDtype...  69 us
    unnamed x1, local copies, waits for them, and re-layouts  2.16 us

profile of v3, /device:TPU:0, one launch (start us, length us, event | category | flops | bytes accessed | tf_op | source)
XLA Modules:
  0.0 73.6 jit_solution(13741129215155546152)
XLA Ops:
  0.6 69.0 %step.1 = (bf16[128,3584]{1,0:T(8,128)(2,1)}, f32[1,1]{1,0:T(1,128)}) custom-call(s32[1,4]{1,0:T(1,128)} %counts_ref.1, s32[1,4]{1,0:T(1,128)} %order_ref.1, bf16[1,1,272,1152]{3,2,1,0:T(8,128)(2,1)} %patches_ref.1, bf16[864,4608]{1,0:T(8,128)(2,1)} %bitcast.3, bf16[2,1,864,3584]{3,2,1,0:T(8,128)(2,1)} %w2_hbm.1, s32[8,128]{1,0:T(8,128)} %bitcast.4, ...), custom_call_target="tpu_custom_call" | custom-call | tf_op jit(solution)/shard_map/step/pallas_call | solution.py:416
  69.6 2.2 %copy.15 = bf16[128,3584]{1,0:T(8,128)(2,1)} copy(bf16[128,3584]{1,0:T(8,128)(2,1)} %get-tuple-element.4) | data formatting | bytes 1835008
